TPU v7x, 128 devices: a whole 4x4x4 slice. The times are simulated.
128 devices in a mesh: blk: 16 (over y_hi, x, core), kv: 8 (over z, y_lo).
Axes of the slice: x: 4, y: 4 (y_hi: 2, y_lo: 2; y = y_hi * 2 + y_lo), z: 4, core: 2. Of those that a mesh axis runs over, the one named last changes fastest.
Arguments:
- tokens: bfloat16 [8192, 2560], P('blk'), may hold values from -6 to 6
- attn_gain: float32 [2560], replicated, may hold values from 0.1 to 1.9
- mlp_gain: float32 [2560], replicated, may hold values from 0.1 to 1.9
- w_query: float32 [2560, 2560], P(('blk', 'kv')), may hold values from -0.375 to 0.375
- w_key: float32 [2560, 640], P(('blk', 'kv')), may hold values from -0.125 to 0.125
- w_value: float32 [2560, 640], P(('blk', 'kv')), may hold values from -0.125 to 0.125
- w_gate: float32 [2560, 6912], P(('blk', 'kv')), may hold values from -0.125 to 0.125
- w_up: float32 [2560, 6912], P(('blk', 'kv')), may hold values from -0.125 to 0.125
- w_out: bfloat16 [2560, 2560], P('kv'), may hold values from -0.125 to 0.125
- w_down: bfloat16 [6912, 2560], P('kv'), may hold values from -0.078125 to 0.078125
- cache: bfloat16 [2, 128, 8, 80, 128], P(None, 'blk', 'kv'), may hold values from -300 to 300
- slot_prompt: int32 [128], replicated, may hold values from 0 to 15, as said below
- prefix_len: int32 [16], replicated, may hold values from 1 to 4096, as said below
- new_len: int32 [16], replicated, may hold values from 256 to 512, as said below
Outputs:
- mixed: bfloat16 [8192, 2560], P('blk', 'kv')
Inputs may be any that keep to these rules, and one draw needn't show every extreme that they name: `slot_prompt`: the 8 slots of one index of blk hold at most 2 blocks of one prompt. One prompt, drawn afresh, has exactly 2 blocks on every index of blk; the other 6 slots of an index hold blocks of distinct prompts; every prompt has at least one block. `prefix_len`: A prompt with c slots has a prefix longer than (c - 1) * 128 and at most c * 128. Rows i >= new_len[p] of prompt p are padding.
All inputs are finite; a program needn't handle non-finite values.
Results may differ from a plain program's by a relative error of at most 0.019.
The roundings to bfloat16 on the way count: a program that leaves them out, or rounds other values in their place, can miss the bound.
Values may be sent and summed in bfloat16 or wider, within the bound.
A program may use at most 128 MiB of HBM per device.

v0:
```python
import math
import jax
import jax.numpy as jnp
from jax import lax
from jax.sharding import PartitionSpec as P

HEADS = 32
KV_HEADS = 8
HD = 80
WINDOW = 4096
SINKS = 4
BLOCK = 128
CAP = 2
FLOOR_SCORE = -1e30
EPSILON = 1e-05
ROPE_BASE = 10000.0


def rms_scale(row_data, gain_vec):
    values = row_data.astype(jnp.float32)
    mean_square = jnp.mean(values * values, axis=-1, keepdims=True)
    return (values * lax.rsqrt(mean_square + EPSILON) * gain_vec).astype(jnp.bfloat16)


def rotate(values, positions):
    head_width = values.shape[-1]
    half_width = head_width // 2
    frequency = ROPE_BASE ** (-2.0 * jnp.arange(half_width, dtype=jnp.float32) / head_width)
    angles = positions.astype(jnp.float32)[:, None] * frequency[None, :]
    cosine = jnp.cos(angles)[:, None, :]
    sine_wave = jnp.sin(angles)[:, None, :]
    first_half = values[..., :half_width]
    second_half = values[..., half_width:]
    return jnp.concatenate(
        [
            first_half * cosine - second_half * sine_wave,
            second_half * cosine + first_half * sine_wave,
        ],
        axis=-1,
    )


def slot_ranks(slot_prompt, prompts, slots):
    onehot = (slot_prompt[:, None] == jnp.arange(prompts, dtype=jnp.int32)[None, :]).astype(
        jnp.int32
    )
    running = jnp.cumsum(onehot, axis=0)
    global_rank = jnp.sum(onehot * (running - 1), axis=1)
    local_count = jnp.cumsum(onehot.reshape(-1, slots, prompts), axis=1).reshape(-1, prompts)
    local_rank = jnp.sum(onehot * (local_count - 1), axis=1)
    return (global_rank, local_rank)


def visible(query_pos, key_pos):
    distance = query_pos - key_pos
    return (distance >= 0) & ((distance < WINDOW) | (key_pos < SINKS))


def partial_block(scores, seen_mask):
    masked = jnp.where(seen_mask, scores, FLOOR_SCORE)
    row_max = jnp.max(masked, axis=-1)
    weights = jnp.where(seen_mask, jnp.exp(masked - row_max[..., None]), 0.0)
    return (row_max, jnp.sum(weights, axis=-1), weights.astype(jnp.bfloat16))


def combine(first_part, second_part):
    maxima = jnp.maximum(first_part[0], second_part[0])
    scale_first = jnp.exp(first_part[0] - maxima)
    scale_second = jnp.exp(second_part[0] - maxima)
    totals = first_part[1] * scale_first + second_part[1] * scale_second
    outputs = first_part[2] * scale_first[..., None] + second_part[2] * scale_second[..., None]
    return (maxima, totals, outputs)


def pack_groups(matrices, groups):
    pieces = [
        matrix.reshape(matrix.shape[0], groups, matrix.shape[1] // groups) for matrix in matrices
    ]
    joined = jnp.concatenate(pieces, axis=2)
    return joined.reshape(matrices[0].shape[0], -1).astype(jnp.bfloat16)


def restack(moved_rows, groups, n_blocks):
    columns = moved_rows.shape[1]
    ordered = moved_rows.reshape(groups, n_blocks, -1, columns)
    return jnp.transpose(ordered, (1, 0, 2, 3)).reshape(-1, columns)


def shards(
    tokens,
    attn_gain,
    mlp_gain,
    w_query,
    w_key,
    w_value,
    w_gate,
    w_up,
    w_out,
    w_down,
    cache,
    slot_prompt,
    prefix_len,
    new_len,
):
    groups = lax.axis_size("kv")
    n_blocks = lax.axis_size("blk")
    blk_index = lax.axis_index("blk")
    kv_index = lax.axis_index("kv")
    merged_attn = pack_groups((w_query, w_key, w_value), groups)
    merged_mlp = pack_groups((w_gate, w_up), groups)
    collected = (
        lax.all_gather(merged_attn, "blk", axis=0, tiled=True),
        lax.all_gather(merged_mlp, "blk", axis=0, tiled=True),
    )
    moved_attn, moved_mlp = (
        lax.all_to_all(collected[0], "kv", split_axis=1, concat_axis=0, tiled=True),
        lax.all_to_all(collected[1], "kv", split_axis=1, concat_axis=0, tiled=True),
    )
    w_qkv = restack(moved_attn, groups, n_blocks)
    w_pair = restack(moved_mlp, groups, n_blocks)
    query_width = w_query.shape[1] // groups
    key_width = w_key.shape[1] // groups
    kv_local = key_width // HD
    per_group = HEADS // KV_HEADS
    new_rows = tokens.shape[0]
    prompts = prefix_len.shape[0]
    slots = cache.shape[1]
    score_scale = 1.0 / math.sqrt(HD)
    prefix_here = prefix_len[blk_index]
    live_count = new_len[blk_index]
    row_ids = jnp.arange(new_rows, dtype=jnp.int32)
    positions = prefix_here + row_ids
    offsets = jnp.arange(BLOCK, dtype=jnp.int32)
    normed = rms_scale(tokens, attn_gain)
    projected = jnp.dot(normed, w_qkv, preferred_element_type=jnp.float32)
    queries = rotate(projected[:, :query_width].reshape(new_rows, -1, HD), positions).astype(
        jnp.bfloat16
    )
    key_new = rotate(
        projected[:, query_width : query_width + key_width].reshape(new_rows, kv_local, HD),
        positions,
    ).astype(jnp.bfloat16)
    value_new = (
        projected[:, query_width + key_width :].reshape(new_rows, kv_local, HD).astype(jnp.bfloat16)
    )
    grouped_q = queries.reshape(new_rows, kv_local, per_group, HD)
    own_scores = (
        jnp.einsum("qgnd,kgd->gnqk", grouped_q, key_new, preferred_element_type=jnp.float32)
        * score_scale
    )
    own_mask = (row_ids[None, :] < live_count) & visible(positions[:, None], positions[None, :])
    own_max, own_sum, own_weights = partial_block(own_scores, own_mask)
    own_out = jnp.einsum(
        "gnqk,kgd->gnqd", own_weights, value_new, preferred_element_type=jnp.float32
    )
    running = (own_max, own_sum, own_out)
    global_rank, local_rank = slot_ranks(slot_prompt, prompts, slots)
    own_prompts = lax.dynamic_slice_in_dim(slot_prompt, blk_index * slots, slots)
    own_ranks = lax.dynamic_slice_in_dim(local_rank, blk_index * slots, slots)
    placed = own_prompts * CAP + own_ranks
    buffer_ids = jnp.arange(prompts * CAP, dtype=jnp.int32)
    matches = placed[None, :] == buffer_ids[:, None]
    source_slot = jnp.sum(
        jnp.where(matches, jnp.arange(slots, dtype=jnp.int32)[None, :], 0), axis=1
    )
    filled = jnp.any(matches, axis=1)
    outgoing = jnp.where(
        filled[None, :, None, None, None],
        jnp.take(cache, source_slot, axis=1),
        jnp.zeros((), cache.dtype),
    )
    arrived = lax.all_to_all(outgoing, "blk", split_axis=1, concat_axis=1, tiled=True)
    slot_ids = jnp.arange(prompts * slots, dtype=jnp.int32)
    landing = slot_ids // slots * CAP + local_rank
    for_me = slot_prompt == blk_index
    received = (landing[None, :] == buffer_ids[:, None]) & for_me[None, :]
    block_number = jnp.sum(jnp.where(received, global_rank[None, :], 0), axis=1)
    block_live = jnp.any(received, axis=1)
    total_slots = prompts * CAP
    group_slots = min(total_slots, max(1, 512 // BLOCK))
    step_count = total_slots // group_slots
    key_blocks = arrived[0].reshape(step_count, group_slots, kv_local, HD, BLOCK)
    value_blocks = arrived[1].reshape(step_count, group_slots, kv_local, HD, BLOCK)
    numbers = block_number.reshape(step_count, group_slots)
    live_flags = block_live.reshape(step_count, group_slots)

    def prefix_step(running_state, inputs):
        key_part, value_part, number_part, flag_part = inputs
        scores = (
            jnp.einsum("qgnd,sgdt->gnqst", grouped_q, key_part, preferred_element_type=jnp.float32)
            * score_scale
        )
        scores = scores.reshape(kv_local, per_group, new_rows, group_slots * BLOCK)
        key_pos = number_part[:, None] * BLOCK + offsets[None, :]
        key_live = (flag_part[:, None] & (key_pos < prefix_here)).reshape(-1)
        seen_mask = key_live[None, :] & visible(positions[:, None], key_pos.reshape(-1)[None, :])
        block_max, block_sum, weights = partial_block(scores, seen_mask)
        weights = weights.reshape(kv_local, per_group, new_rows, group_slots, BLOCK)
        block_out = jnp.einsum(
            "gnqst,sgdt->gnqd", weights, value_part, preferred_element_type=jnp.float32
        )
        return (combine(running_state, (block_max, block_sum, block_out)), None)

    running = lax.scan(prefix_step, running, (key_blocks, value_blocks, numbers, live_flags))[0]
    totals = running[1]
    outputs = running[2]
    attended = (
        jnp.transpose(outputs / totals[..., None], (2, 0, 1, 3))
        .reshape(new_rows, -1)
        .astype(jnp.bfloat16)
    )
    projected_out = jnp.dot(attended, w_out, preferred_element_type=jnp.float32)
    summed = lax.psum(projected_out.astype(jnp.bfloat16), "kv").astype(jnp.float32)
    middle = (tokens.astype(jnp.float32) + summed).astype(jnp.bfloat16)
    normed_mid = rms_scale(middle, mlp_gain)
    paired = jnp.dot(normed_mid, w_pair, preferred_element_type=jnp.float32)
    hidden_width = w_pair.shape[1] // 2
    hidden = (jax.nn.silu(paired[:, :hidden_width]) * paired[:, hidden_width:]).astype(jnp.bfloat16)
    down_part = jnp.dot(hidden, w_down, preferred_element_type=jnp.float32)
    reduced = lax.psum_scatter(
        down_part.astype(jnp.bfloat16), "kv", scatter_dimension=1, tiled=True
    ).astype(jnp.float32)
    out_width = reduced.shape[1]
    residual = lax.dynamic_slice_in_dim(middle, kv_index * out_width, out_width, 1).astype(
        jnp.float32
    )
    mixed = jnp.where((row_ids < live_count)[:, None], residual + reduced, 0.0)
    return mixed.astype(jnp.bfloat16)


def solution(mesh):
    return jax.shard_map(
        shards,
        mesh=mesh,
        in_specs=(
            P("blk", None),
            P(),
            P(),
            P(("blk", "kv"), None),
            P(("blk", "kv"), None),
            P(("blk", "kv"), None),
            P(("blk", "kv"), None),
            P(("blk", "kv"), None),
            P("kv", None),
            P("kv", None),
            P(None, "blk", "kv", None, None),
            P(),
            P(),
            P(),
        ),
        out_specs=P("blk", "kv"),
        check_vma=False,
    )
```

profile of v0, /device:TPU:1, one launch (start us, length us, event | category | flops | bytes accessed | tf_op | source)
XLA Modules:
  0.0 535.5 jit_solution(12732997169242167067)
XLA Ops:
  18.9 8.4 %all-to-all-start.1 = ((bf16[2,32,1,80,128]{4,3,0,2,1:T(8,128)(2,1)}), bf16[2,32,1,80,128]{4,3,0,2,1:T(8,128)(2,1)S(1)}, u32[]{:S(2)}, u32[]{:S(2)}) async-start(bf16[2,32,1,80,128]{4,3,0,2,1:T(8,128)(2,1)} %fusion.68), calls=%async_computation.1 | async-start | bytes 2621440 | tf_op jit(solution)/shard_map/all_to_all | solution.py:172
  27.4 41.5 %all-gather.5.cloned.1.call-done = bf16[16,20,3840]{2,1,0:T(8,128)(2,1)} async-done(((bf16[1,20,3840]{2,1,0:T(8,128)(2,1)}), bf16[16,20,3840]{2,1,0:T(8,128)(2,1)}) %all-gather.5.cloned.1.call-update) | async-done | bytes 2457616 | tf_op jit(solution)/shard_map/all_gather | solution.py:112
  68.9 6.6 %all_to_all.27 = bf16[320,8,480]{2,1,0:T(8,128)(2,1)} reshape(bf16[16,20,3840]{2,1,0:T(8,128)(2,1)} %all-gather.5.cloned.1.call-done) | data formatting | bytes 4915200 | tf_op jit(solution)/shard_map/all_to_all | solution.py:116
  75.4 4.2 copy.61
  79.6 4.7 all-to-all-start
  85.6 4.4 copy.60
  97.2 29.5 %all-to-all-done = bf16[320,8,480]{2,0,1:T(8,128)(2,1)} async-done(((bf16[320,8,480]{2,0,1:T(8,128)(2,1)}), bf16[320,8,480]{2,0,1:T(8,128)(2,1)}, u32[]{:S(2)}, u32[]{:S(2)}) %all-to-all-start) | async-done | bytes 2457632 | tf_op jit(solution)/shard_map/all_to_all | solution.py:116
  126.7 3.3 copy.62
  132.9 5.5 %reshape.470 = bf16[2560,480]{1,0:T(8,128)(2,1)} reshape(bf16[16,8,20,480]{3,2,1,0:T(8,128)(2,1)} %copy.63) | data formatting | bytes 4915200 | tf_op jit(solution)/shard_map/reshape | solution.py:86
  138.4 4.2 fusion.55
  146.5 16.6 %all-gather.7.cloned.1.call-done = bf16[16,20,13824]{2,1,0:T(8,128)(2,1)} async-done(((bf16[1,20,13824]{2,1,0:T(8,128)(2,1)}), bf16[16,20,13824]{2,1,0:T(8,128)(2,1)}) %all-gather.7.cloned.1.call-update) | async-done | bytes 8847376 | tf_op jit(solution)/shard_map/all_gather | solution.py:113
  163.1 16.9 %all_to_all.31 = bf16[320,8,1728]{2,1,0:T(8,128)(2,1)} reshape(bf16[16,20,13824]{2,1,0:T(8,128)(2,1)} %all-gather.7.cloned.1.call-done) | data formatting | bytes 17694720 | tf_op jit(solution)/shard_map/all_to_all | solution.py:117
  180.0 8.9 %copy.68 = bf16[320,8,1728]{2,0,1:T(8,128)(2,1)} copy(bf16[320,8,1728]{2,1,0:T(8,128)(2,1)} %all_to_all.31) | data formatting | bytes 17694720 | tf_op jit(solution)/shard_map/all_to_all | solution.py:117
  189.0 5.0 all-to-all-start.2
  194.0 57.9 %while.16 = (s32[]{:T(128)}, f32[1,4,512]{2,1,0:T(4,128)S(1)}, f32[1,4,512]{2,1,0:T(4,128)S(1)}, f32[1,4,512,80]{2,3,1,0:T(8,128)S(1)}, pred[8,4]{1,0:T(8,128)(4...) while((s32[]{:T(128)}, f32[1,4,512]{2,1,0:T(4,128)S(1)}, ...), condition=%wide.region_14.15_spmd.clone.clone, body=%wide.region_11.14_spmd.clone.clone.sunk | while | flops 351253504 | bytes 15599833 | solution.py:204
  252.0 3.1 convolution_convert_fusion.1
  255.3 151.3 %all-reduce.2.cloned.1.call-done = bf16[512,2560]{0,1:T(8,128)(2,1)} async-done(((bf16[512,2560]{0,1:T(8,128)(2,1)}), bf16[512,2560]{0,1:T(8,128)(2,1)}) %all-reduce.2.cloned.1.call-update) | async-done | bytes 2621456 | tf_op jit(solution)/shard_map/psum | solution.py:213
  406.6 5.1 fusion.44
  411.7 12.2 %copy.69 = bf16[320,8,1728]{2,1,0:T(8,128)(2,1)} copy(bf16[320,8,1728]{2,0,1:T(8,128)(2,1)} %all-to-all-done.2) | data formatting | bytes 17694720 | tf_op jit(solution)/shard_map/all_to_all | solution.py:117
  423.9 10.4 %copy.70 = bf16[16,8,20,1728]{3,2,1,0:T(8,128)(2,1)} copy(bf16[16,8,20,1728]{3,1,2,0:T(8,128)(2,1)} %bitcast.203) | data formatting | bytes 17694720 | tf_op jit(solution)/shard_map/transpose | solution.py:86
  434.3 14.4 %reshape.479 = bf16[2560,1728]{1,0:T(8,128)(2,1)} reshape(bf16[16,8,20,1728]{3,2,1,0:T(8,128)(2,1)} %copy.70) | data formatting | bytes 17694720 | tf_op jit(solution)/shard_map/reshape | solution.py:86
  448.6 8.9 %fusion.57 = f32[512,1728]{0,1:T(8,128)S(1)} fusion(bf16[2560,1728]{1,0:T(8,128)(2,1)} %reshape.479, bf16[512,2560]{0,1:T(8,128)(2,1)} %get-tuple-element.184, f32[2560]{0:T(1024)S(1)} %copy-done.4, f32[512]{0:T(512)S(1)} %add_rsqrt_fusion), kind=kOutput, calls=%fused_computation.68 | convolution fusion | flops 4535091200 | bytes 15020032 | tf_op jit(solution)/shard_map/dot_general | solution.py:216
  457.5 7.4 %fusion.51 = bf16[2560,512]{1,0:T(8,128)(2,1)} fusion(bf16[864,2560]{1,0:T(8,128)(2,1)} %param.25, f32[512,1728]{0,1:T(8,128)S(1)} %fusion.57), kind=kOutput, calls=%fused_computation.63 | convolution fusion | flops 2268889088 | bytes 10584064 | tf_op jit(solution)/shard_map/dot_general | solution.py:219
  465.0 61.9 %reduce-scatter.4.cloned.1.call-done = bf16[320,512]{1,0:T(8,128)(2,1)} async-done(((bf16[2560,512]{1,0:T(8,128)(2,1)}), bf16[320,512]{1,0:T(8,128)(2,1)}) %reduce-scatter.4.cloned.1.call-update) | async-done | bytes 327696
  (178 shorter events, 87.0 us)
Async XLA Ops:
  6.5 245.4 %copy-start = (bf16[320,2560]{1,0:T(8,128)(2,1)S(1)}, bf16[320,2560]{1,0:T(8,128)(2,1)}, u32[]{:S(2)}) copy-start(bf16[320,2560]{1,0:T(8,128)(2,1)} %param.24) | copy-start | bytes 4915204
  6.5 9.2 %copy-start.2 = (s32[128]{0:T(128)S(1)}, s32[128]{0:T(128)}, u32[]{:S(2)}) copy-start(s32[128]{0:T(128)} %param.27) | copy-start | bytes 1540
  6.5 62.3 %all-gather.5.cloned.1.call-start = ((), (), s32[]{:S(2)}) async-start(), calls=%async_computation.5 | async-start | bytes 3133440 | tf_op jit(solution)/shard_map/all_gather | solution.py:112
  7.5 9.2 %copy-start.1 = (bf16[2,8,1,80,128]{4,3,2,1,0:T(8,128)(2,1)S(1)}, bf16[2,8,1,80,128]{4,3,2,1,0:T(8,128)(2,1)}, u32[]{:S(2)}) copy-start(bf16[2,8,1,80,128]{4,3,2,1,0:T(8,128)(2,1)} %param.26) | copy-start | bytes 983044
  10.8 152.4 %all-gather.7.cloned.1.call-start = ((), (), s32[]{:S(2)}) async-start(), calls=%async_computation.6 | async-start | bytes 11280384 | tf_op jit(solution)/shard_map/all_gather | solution.py:113
  18.9 60.7 %all-to-all-start.1 = ((bf16[2,32,1,80,128]{4,3,0,2,1:T(8,128)(2,1)}), bf16[2,32,1,80,128]{4,3,0,2,1:T(8,128)(2,1)S(1)}, u32[]{:S(2)}, u32[]{:S(2)}) async-start(bf16[2,32,1,80,128]{4,3,0,2,1:T(8,128)(2,1)} %fusion.68), calls=%async_computation.1 | async-start | bytes 2621440 | tf_op jit(solution)/shard_map/all_to_all | solution.py:172
  75.4 8.9 %copy-start.5 = (s32[16]{0:T(128)S(1)}, s32[16]{0:T(128)}, u32[]{:S(2)}) copy-start(s32[16]{0:T(128)} %param.28) | copy-start | bytes 196
  75.4 9.6 %copy-start.6 = (s32[16]{0:T(128)S(1)}, s32[16]{0:T(128)}, u32[]{:S(2)}) copy-start(s32[16]{0:T(128)} %param.29) | copy-start | bytes 196
  79.6 47.1 %all-to-all-start = ((bf16[320,8,480]{2,0,1:T(8,128)(2,1)}), bf16[320,8,480]{2,0,1:T(8,128)(2,1)}, u32[]{:S(2)}, u32[]{:S(2)}) async-start(bf16[320,8,480]{2,0,1:T(8,128)(2,1)} %copy.61), calls=%async_computation | async-start | bytes 5242880 | tf_op jit(solution)/shard_map/all_to_all | solution.py:116
  132.9 5.5 %copy-start.3 = (f32[2560]{0:T(1024)S(1)}, f32[2560]{0:T(1024)}, u32[]{:S(2)}) copy-start(f32[2560]{0:T(1024)} %param.17) | copy-start | bytes 30724
  189.0 222.7 %all-to-all-start.2 = ((bf16[320,8,1728]{2,0,1:T(8,128)(2,1)}), bf16[320,8,1728]{2,0,1:T(8,128)(2,1)}, u32[]{:S(2)}, u32[]{:S(2)}) async-start(bf16[320,8,1728]{2,0,1:T(8,128)(2,1)} %copy.68), calls=%async_computation.2 | async-start | bytes 18350080 | tf_op jit(solution)/shard_map/all_to_all | solution.py:117
  194.0 212.6 %all-reduce.2.cloned.1.call-start = ((), (), s32[]{:S(2)}) async-start(), calls=%async_computation.4 | async-start | bytes 5242880 | tf_op jit(solution)/shard_map/psum | solution.py:213
  255.1 271.7 %reduce-scatter.4.cloned.1.call-start = ((), (), s32[]{:S(2)}) async-start(), calls=%async_computation.7 | async-start | bytes 2949120
  434.3 14.4 %copy-start.4 = (f32[2560]{0:T(1024)S(1)}, f32[2560]{0:T(1024)}, u32[]{:S(2)}) copy-start(f32[2560]{0:T(1024)} %param.18) | copy-start | bytes 30724
Sparse Core Ops, SparseCore 0:
  10.9 57.9 all-gather.4
  71.3 91.7 all-gather.6
  255.2 151.3 all-reduce.1
  465.1 61.6 reduce-scatter.3
where the time goes:
time: 543 us; the launch traced here: 536 us
  waiting for transfers between devices  301 us (55%)
  local copies, waits for them, and re-layouts  97.1 us (18%)
  matrix products  58.8 us (11%)
  other arithmetic  46.1 us (8%)
  starting transfers between devices  18.5 us (3%)
  between operations  13.6 us (3%)
    psum x1, waiting for transfers between devices, shards(): lax.psum(projected_out.astype(jnp.bfloat16), 'kv').astype(jnp.float32)  151 us
    unnamed x5, waiting for transfers between devices  61.9 us
    all_gather x1, waiting for transfers between devices, shards(): lax.all_gather(merged_attn, 'blk', axis=0, tiled=True)  41.5 us
    all_to_all x3, local copies, waits for them, and re-layouts, shards(): lax.all_to_all(collected[1], 'kv', split_axis=1, concat_axis=0, tiled=True)  38 us
    all_to_all x1, waiting for transfers between devices, shards(): lax.all_to_all(collected[0], 'kv', split_axis=1, concat_axis=0, tiled=True)  29.5 us
    reshape x2, local copies, waits for them, and re-layouts, restack(): return jnp.transpose(ordered, (1, 0, 2, 3)).reshape(-1, columns)  19.9 us
    dot_general x8, matrix products, prefix_step(): jnp.einsum('gnqst,sgdt->gnqd', weights, value_part, preferred_element_typ...  18.6 us
    all_gather x1, waiting for transfers between devices, shards(): lax.all_gather(merged_mlp, 'blk', axis=0, tiled=True)  16.6 us
  transfers between devices with their start and end apart: 7, of which 5 were waited for; matrix products, arithmetic and copies ran while one was open for 21% of the time, Pallas kernels for 0%

commit v1 on v0

--- a/solution.py
+++ b/solution.py
@@ -109,7 +109,9 @@
     merged_attn = pack_groups((w_query, w_key, w_value), groups)
     merged_mlp = pack_groups((w_gate, w_up), groups)
     collected = (
-        lax.all_gather(merged_attn, "blk", axis=0, tiled=True),
+        jnp.concatenate(
+            lax.all_to_all(jnp.stack([merged_attn] * lax.axis_size("blk")), "blk", 0, 0), axis=0
+        ),
         lax.all_gather(merged_mlp, "blk", axis=0, tiled=True),
     )
     moved_attn, moved_mlp = (

time: 543 us -> 556 us (1.024)
  starting transfers between devices: 18.5 us -> 29.3 us
    all_to_all x0 -> x1, waiting for transfers between devices: none -> 41.8 us  [shards(): lax.all_to_all(jnp.stack([merged_attn] * lax.axis_size('blk')), 'blk', 0, 0)]
    all_gather x1 -> x0, waiting for transfers between devices: 41.5 us -> none  [shards(): lax.all_gather(merged_attn, 'blk', axis=0, tiled=True)]
    all_gather x1, waiting for transfers between devices: 16.6 us -> 0.02 us  [shards(): lax.all_gather(merged_mlp, 'blk', axis=0, tiled=True)]
    all_to_all x1, waiting for transfers between devices: 0.01 us -> 13.5 us  [shards(): lax.all_to_all(outgoing, 'blk', split_axis=1, concat_axis=1, tiled=True)]
    all_to_all x0 -> x1, starting transfers between devices: none -> 8.45 us  [shards(): lax.all_to_all(jnp.stack([merged_attn] * lax.axis_size('blk')), 'blk', 0, 0)]
    unnamed x5 -> x4, waiting for transfers between devices: 61.9 us -> 61.8 us
  transfers between devices with their start and end apart: 7 -> 7, of which waited for: 5 -> 5; matrix products, arithmetic and copies ran while one was open for 21% -> 20% of each run, Pallas kernels for 0% -> 0%
where the time goes in v1:
time: 556 us; the launch traced here: 549 us
  waiting for transfers between devices  303 us (54%)
  local copies, waits for them, and re-layouts  98.3 us (18%)
  matrix products  58.8 us (11%)
  other arithmetic  43.5 us (8%)
  starting transfers between devices  29.3 us (5%)
  between operations  15.4 us (3%)
    psum x1, waiting for transfers between devices, shards(): lax.psum(projected_out.astype(jnp.bfloat16), 'kv').astype(jnp.float32)  155 us
    unnamed x4, waiting for transfers between devices  61.8 us
    all_to_all x1, waiting for transfers between devices, shards(): lax.all_to_all(jnp.stack([merged_attn] * lax.axis_size('blk')), 'blk', 0, 0)  41.8 us
    all_to_all x3, local copies, waits for them, and re-layouts, shards(): lax.all_to_all(collected[1], 'kv', split_axis=1, concat_axis=0, tiled=True)  38 us
    all_to_all x1, waiting for transfers between devices, shards(): lax.all_to_all(collected[0], 'kv', split_axis=1, concat_axis=0, tiled=True)  30.8 us
    reshape x2, local copies, waits for them, and re-layouts, restack(): return jnp.transpose(ordered, (1, 0, 2, 3)).reshape(-1, columns)  19.9 us
    dot_general x8, matrix products, prefix_step(): jnp.einsum('gnqst,sgdt->gnqd', weights, value_part, preferred_element_typ...  18.6 us
    dot_general x8, matrix products, prefix_step(): jnp.einsum('qgnd,sgdt->gnqst', grouped_q, key_part, preferred_element_typ...  14.3 us
  transfers between devices with their start and end apart: 7, of which 5 were waited for; matrix products, arithmetic and copies ran while one was open for 20% of the time, Pallas kernels for 0%

profile of v1, /device:TPU:1, one launch (start us, length us, event | category | flops | bytes accessed | tf_op | source)
XLA Modules:
  0.0 548.6 jit_solution(3816590424289516098)
XLA Ops:
  15.1 8.4 %all-to-all-start = ((bf16[16,20,3840]{2,1,0:T(8,128)(2,1)}), bf16[16,20,3840]{2,1,0:T(8,128)(2,1)}, u32[]{:S(2)}, u32[]{:S(2)}) async-start(bf16[16,20,3840]{2,1,0:T(8,128)(2,1)} %stack.2), calls=%async_computation | async-start | bytes 5898240 | tf_op jit(solution)/shard_map/all_to_all | solution.py:113
  26.8 41.8 %all-to-all-done = bf16[16,20,3840]{2,1,0:T(8,128)(2,1)} async-done(((bf16[16,20,3840]{2,1,0:T(8,128)(2,1)}), bf16[16,20,3840]{2,1,0:T(8,128)(2,1)}, u32[]{:S(2)}, u32[]{:S(2)}) %all-to-all-start) | async-done | bytes 2457632 | tf_op jit(solution)/shard_map/all_to_all | solution.py:113
  68.5 7.9 %all-to-all-start.2 = ((bf16[2,32,1,80,128]{4,3,0,2,1:T(8,128)(2,1)}), bf16[2,32,1,80,128]{4,3,0,2,1:T(8,128)(2,1)S(1)}, u32[]{:S(2)}, u32[]{:S(2)}) async-start(bf16[2,32,1,80,128]{4,3,0,2,1:T(8,128)(2,1)} %fusion.68), calls=%async_computation.2 | async-start | bytes 2621440 | tf_op jit(solution)/shard_map/all_to_all | solution.py:174
  76.4 6.7 %all_to_all.31 = bf16[320,8,480]{2,1,0:T(8,128)(2,1)} reshape(bf16[16,20,3840]{2,1,0:T(8,128)(2,1)} %all-to-all-done) | data formatting | bytes 4915200 | tf_op jit(solution)/shard_map/all_to_all | solution.py:118
  83.1 4.2 copy.61
  87.2 13.5 %all-to-all-done.2 = bf16[2,32,1,80,128]{4,3,0,2,1:T(8,128)(2,1)S(1)} async-done(((bf16[2,32,1,80,128]{4,3,0,2,1:T(8,128)(2,1)}), bf16[2,32,1,80,128]{4,3,0,2,1:T(8,128)(2,1)S(1)}, u32[]{:S(2)}, u32[]{:S(2)}) %all-to-all-start.2) | async-done | bytes 1310752 | tf_op jit(solution)/shard_map/all_to_all | solution.py:174
  100.7 7.7 %all-to-all-start.1 = ((bf16[320,8,480]{2,0,1:T(8,128)(2,1)}), bf16[320,8,480]{2,0,1:T(8,128)(2,1)}, u32[]{:S(2)}, u32[]{:S(2)}) async-start(bf16[320,8,480]{2,0,1:T(8,128)(2,1)} %copy.61), calls=%async_computation.1 | async-start | bytes 5242880 | tf_op jit(solution)/shard_map/all_to_all | solution.py:118
  109.7 4.4 copy.60
  121.3 30.8 %all-to-all-done.1 = bf16[320,8,480]{2,0,1:T(8,128)(2,1)} async-done(((bf16[320,8,480]{2,0,1:T(8,128)(2,1)}), bf16[320,8,480]{2,0,1:T(8,128)(2,1)}, u32[]{:S(2)}, u32[]{:S(2)}) %all-to-all-start.1) | async-done | bytes 2457632 | tf_op jit(solution)/shard_map/all_to_all | solution.py:118
  152.2 3.2 copy.62
  158.2 5.5 %reshape.475 = bf16[2560,480]{1,0:T(8,128)(2,1)} reshape(bf16[16,8,20,480]{3,2,1,0:T(8,128)(2,1)} %copy.63) | data formatting | bytes 4915200 | tf_op jit(solution)/shard_map/reshape | solution.py:86
  163.8 4.2 fusion.55
  171.9 16.9 %all_to_all.35 = bf16[320,8,1728]{2,1,0:T(8,128)(2,1)} reshape(bf16[16,20,13824]{2,1,0:T(8,128)(2,1)} %all-gather.3.cloned.1.call-done) | data formatting | bytes 17694720 | tf_op jit(solution)/shard_map/all_to_all | solution.py:119
  188.8 8.9 %copy.68 = bf16[320,8,1728]{2,0,1:T(8,128)(2,1)} copy(bf16[320,8,1728]{2,1,0:T(8,128)(2,1)} %all_to_all.35) | data formatting | bytes 17694720 | tf_op jit(solution)/shard_map/all_to_all | solution.py:119
  197.8 5.0 all-to-all-start.3
  202.8 57.9 %while.16 = (s32[]{:T(128)}, f32[1,4,512]{2,1,0:T(4,128)S(1)}, f32[1,4,512]{2,1,0:T(4,128)S(1)}, f32[1,4,512,80]{2,3,1,0:T(8,128)S(1)}, pred[8,4]{1,0:T(8,128)(4...) while((s32[]{:T(128)}, f32[1,4,512]{2,1,0:T(4,128)S(1)}, ...), condition=%wide.region_14.15_spmd.clone.clone, body=%wide.region_11.14_spmd.clone.clone.sunk | while | flops 351253504 | bytes 15599833 | solution.py:206
  264.2 154.8 %all-reduce.2.cloned.1.call-done = bf16[512,2560]{0,1:T(8,128)(2,1)} async-done(((bf16[512,2560]{0,1:T(8,128)(2,1)}), bf16[512,2560]{0,1:T(8,128)(2,1)}) %all-reduce.2.cloned.1.call-update) | async-done | bytes 2621456 | tf_op jit(solution)/shard_map/psum | solution.py:215
  418.9 5.1 fusion.44
  424.0 12.2 %copy.69 = bf16[320,8,1728]{2,1,0:T(8,128)(2,1)} copy(bf16[320,8,1728]{2,0,1:T(8,128)(2,1)} %all-to-all-done.3) | data formatting | bytes 17694720 | tf_op jit(solution)/shard_map/all_to_all | solution.py:119
  436.2 10.4 %copy.70 = bf16[16,8,20,1728]{3,2,1,0:T(8,128)(2,1)} copy(bf16[16,8,20,1728]{3,1,2,0:T(8,128)(2,1)} %bitcast.203) | data formatting | bytes 17694720 | tf_op jit(solution)/shard_map/transpose | solution.py:86
  446.6 14.4 %reshape.484 = bf16[2560,1728]{1,0:T(8,128)(2,1)} reshape(bf16[16,8,20,1728]{3,2,1,0:T(8,128)(2,1)} %copy.70) | data formatting | bytes 17694720 | tf_op jit(solution)/shard_map/reshape | solution.py:86
  461.0 8.9 %fusion.57 = f32[512,1728]{0,1:T(8,128)S(1)} fusion(bf16[2560,1728]{1,0:T(8,128)(2,1)} %reshape.484, bf16[512,2560]{0,1:T(8,128)(2,1)} %get-tuple-element.184, f32[2560]{0:T(1024)S(1)} %copy-done.7, f32[512]{0:T(512)S(1)} %add_rsqrt_fusion), kind=kOutput, calls=%fused_computation.68 | convolution fusion | flops 4535091200 | bytes 15020032 | tf_op jit(solution)/shard_map/dot_general | solution.py:218
  469.8 7.4 %fusion.51 = bf16[2560,512]{1,0:T(8,128)(2,1)} fusion(bf16[864,2560]{1,0:T(8,128)(2,1)} %param.25, f32[512,1728]{0,1:T(8,128)S(1)} %fusion.57), kind=kOutput, calls=%fused_computation.63 | convolution fusion | flops 2268889088 | bytes 10584064 | tf_op jit(solution)/shard_map/dot_general | solution.py:221
  477.3 61.7 %reduce-scatter.4.cloned.1.call-done = bf16[320,512]{1,0:T(8,128)(2,1)} async-done(((bf16[2560,512]{1,0:T(8,128)(2,1)}), bf16[320,512]{1,0:T(8,128)(2,1)}) %reduce-scatter.4.cloned.1.call-update) | async-done | bytes 327696
  (184 shorter events, 88.6 us)
Async XLA Ops:
  7.4 253.4 %copy-start = (bf16[320,2560]{1,0:T(8,128)(2,1)S(1)}, bf16[320,2560]{1,0:T(8,128)(2,1)}, u32[]{:S(2)}) copy-start(bf16[320,2560]{1,0:T(8,128)(2,1)} %param.24) | copy-start | bytes 4915204
  7.4 5.2 copy-start.3
  7.4 5.3 copy-start.4
  7.4 5.4 copy-start.2
  7.4 164.5 %all-gather.3.cloned.1.call-start = ((), (), s32[]{:S(2)}) async-start(), calls=%async_computation.6 | async-start | bytes 11280384 | tf_op jit(solution)/shard_map/all_gather | solution.py:115
  13.3 10.2 %copy-start.5 = (s32[128]{0:T(128)S(1)}, s32[128]{0:T(128)}, u32[]{:S(2)}) copy-start(s32[128]{0:T(128)} %param.27) | copy-start | bytes 1540
  13.4 11.2 %copy-start.1 = (bf16[2,8,1,80,128]{4,3,2,1,0:T(8,128)(2,1)S(1)}, bf16[2,8,1,80,128]{4,3,2,1,0:T(8,128)(2,1)}, u32[]{:S(2)}) copy-start(bf16[2,8,1,80,128]{4,3,2,1,0:T(8,128)(2,1)} %param.26) | copy-start | bytes 983044
  15.1 53.4 %all-to-all-start = ((bf16[16,20,3840]{2,1,0:T(8,128)(2,1)}), bf16[16,20,3840]{2,1,0:T(8,128)(2,1)}, u32[]{:S(2)}, u32[]{:S(2)}) async-start(bf16[16,20,3840]{2,1,0:T(8,128)(2,1)} %stack.2), calls=%async_computation | async-start | bytes 5898240 | tf_op jit(solution)/shard_map/all_to_all | solution.py:113
  68.5 32.2 %all-to-all-start.2 = ((bf16[2,32,1,80,128]{4,3,0,2,1:T(8,128)(2,1)}), bf16[2,32,1,80,128]{4,3,0,2,1:T(8,128)(2,1)S(1)}, u32[]{:S(2)}, u32[]{:S(2)}) async-start(bf16[2,32,1,80,128]{4,3,0,2,1:T(8,128)(2,1)} %fusion.68), calls=%async_computation.2 | async-start | bytes 2621440 | tf_op jit(solution)/shard_map/all_to_all | solution.py:174
  83.1 25.4 %copy-start.8 = (s32[16]{0:T(128)S(1)}, s32[16]{0:T(128)}, u32[]{:S(2)}) copy-start(s32[16]{0:T(128)} %param.28) | copy-start | bytes 196
  83.1 26.1 %copy-start.9 = (s32[16]{0:T(128)S(1)}, s32[16]{0:T(128)}, u32[]{:S(2)}) copy-start(s32[16]{0:T(128)} %param.29) | copy-start | bytes 196
  100.7 51.4 %all-to-all-start.1 = ((bf16[320,8,480]{2,0,1:T(8,128)(2,1)}), bf16[320,8,480]{2,0,1:T(8,128)(2,1)}, u32[]{:S(2)}, u32[]{:S(2)}) async-start(bf16[320,8,480]{2,0,1:T(8,128)(2,1)} %copy.61), calls=%async_computation.1 | async-start | bytes 5242880 | tf_op jit(solution)/shard_map/all_to_all | solution.py:118
  158.2 5.5 %copy-start.6 = (f32[2560]{0:T(1024)S(1)}, f32[2560]{0:T(1024)}, u32[]{:S(2)}) copy-start(f32[2560]{0:T(1024)} %param.17) | copy-start | bytes 30724
  197.8 226.3 %all-to-all-start.3 = ((bf16[320,8,1728]{2,0,1:T(8,128)(2,1)}), bf16[320,8,1728]{2,0,1:T(8,128)(2,1)}, u32[]{:S(2)}, u32[]{:S(2)}) async-start(bf16[320,8,1728]{2,0,1:T(8,128)(2,1)} %copy.68), calls=%async_computation.3 | async-start | bytes 18350080 | tf_op jit(solution)/shard_map/all_to_all | solution.py:119
  202.8 216.1 %all-reduce.2.cloned.1.call-start = ((), (), s32[]{:S(2)}) async-start(), calls=%async_computation.5 | async-start | bytes 5242880 | tf_op jit(solution)/shard_map/psum | solution.py:215
  263.9 275.1 %reduce-scatter.4.cloned.1.call-start = ((), (), s32[]{:S(2)}) async-start(), calls=%async_computation.7 | async-start | bytes 2949120
  446.6 14.4 %copy-start.7 = (f32[2560]{0:T(1024)S(1)}, f32[2560]{0:T(1024)}, u32[]{:S(2)}) copy-start(f32[2560]{0:T(1024)} %param.18) | copy-start | bytes 30724
Sparse Core Ops, SparseCore 0:
  12.6 138.0 all-gather.2
Sparse Core Ops, SparseCore 1:
  264.0 154.9 all-reduce.1
  477.4 61.6 reduce-scatter.3
